TPU v7x, 512 devices: a whole 4x8x8 slice. The times are simulated.
512 devices in a mesh: space: 32 (over y, z_lo), mode: 16 (over z_hi, x, core).
Axes of the slice: x: 4, y: 8, z: 8 (z_hi: 2, z_lo: 4; z = z_hi * 4 + z_lo), core: 2. Of those that a mesh axis runs over, the one named last changes fastest.
Arguments:
- left_modes: bfloat16 [2, 12, 4096, 4096], P(None, None, 'space', 'mode'), may hold values from -6 to 6
- right_modes: bfloat16 [32, 2, 12, 4096], P('mode', None, None, 'space'), may hold values from -6 to 6
- momenta: int32 [16, 3], replicated, may hold values from -2 to 2
- coords: int32 [3, 4096], P(None, 'space'), may hold values from 0 to 95
Outputs:
- meson_field: float32 [4096, 16, 2, 32], P(('mode', 'space'))
All inputs are finite; a program needn't handle non-finite values.
Results may differ from a plain program's by a relative error of at most 0.0028.
Values may be sent and summed in bfloat16 or wider, within the bound.
No kernel may reach another device: no remote copies, remote signals or barrier semaphores. Data moves between devices by JAX's collectives and lax.ppermute only.
A program may use at most 64 MiB of HBM per device.

v0:
```python
import math
import jax
import jax.numpy as jnp
from jax import lax
from jax.sharding import PartitionSpec as P

EXTENT = 96


def phase_tables(momenta, coords):
    phase_turns = jnp.mod(jnp.sum(momenta[:, :, None] * coords[None, :, :], axis=1), EXTENT)
    angles = phase_turns.astype(jnp.float32) * (2.0 * math.pi / EXTENT)
    return (jnp.cos(angles), jnp.sin(angles))


def phased_block(right_piece, cosines, sines):
    piece_rows = right_piece.shape[0]
    real_part = right_piece[:, 0].astype(jnp.float32)[None]
    imag_part = right_piece[:, 1].astype(jnp.float32)[None]
    cos_wide = cosines[:, None, None, :]
    sin_wide = sines[:, None, None, :]
    turned_re = (cos_wide * real_part + sin_wide * imag_part).astype(jnp.bfloat16)
    turned_im = (cos_wide * imag_part - sin_wide * real_part).astype(jnp.bfloat16)
    upper_half = jnp.stack([turned_re, turned_im], axis=2)
    lower_half = jnp.stack([turned_im, -turned_re], axis=2)
    stacked = jnp.stack([upper_half, lower_half], axis=1)
    return stacked.reshape(cosines.shape[0] * 2 * piece_rows, -1)


def tile_terms(left_mat, right_piece, cosines, sines):
    stacked = phased_block(right_piece, cosines, sines)
    product = lax.dot_general(
        stacked, left_mat, (((1,), (0,)), ((), ())), preferred_element_type=jnp.float32
    )
    return product.reshape(cosines.shape[0], 2, right_piece.shape[0], left_mat.shape[1])


def body(left_modes, right_modes, momenta, coords):
    cosines, sines = phase_tables(momenta, coords)
    left_mat = left_modes.reshape(-1, left_modes.shape[-1])
    norm_scale = 1.0 / math.sqrt(12 * coords.shape[1] * lax.axis_size("space"))
    partial_value = tile_terms(
        left_mat, lax.all_gather(right_modes, "mode", axis=0, tiled=True), cosines, sines
    )
    owned = lax.psum_scatter(partial_value, "space", scatter_dimension=3, tiled=True)
    summed = jnp.transpose(owned, (3, 0, 1, 2))
    return summed * norm_scale


def solution(mesh):
    in_specs = (
        P(None, None, "space", "mode"),
        P("mode", None, None, "space"),
        P(),
        P(None, "space"),
    )
    out_specs = P(("mode", "space"), None, None, None)
    return jax.shard_map(body, mesh=mesh, in_specs=in_specs, out_specs=out_specs, check_vma=False)
```

profile of v0, /device:TPU:6, one launch (start us, length us, event | category | flops | bytes accessed | tf_op | source)
XLA Modules:
  0.0 231.0 jit_solution(12125679252218744204)
XLA Ops:
  6.5 0.0 copy-start
  6.5 0.0 reduce-scatter.2.cloned.1.call-start
  6.5 0.9 multiply_reduce_fusion
  7.4 0.1 fusion.13
  7.5 27.4 %all_gather.3 = bf16[32,2,12,128]{3,1,2,0:T(2,128)(2,1)S(1)} all-gather(bf16[2,2,12,128]{3,1,2,0:T(2,128)(2,1)} %param.5), channel_id=1, replica_groups=mesh['space'=32,'mode'=16] {'mode'}, dimensions={0}, use_global_device_ids=true | all-gather | bytes 208896 | tf_op jit(solution)/shard_map/all_gather | solution.py:43
  34.9 0.3 fusion.16
  35.2 0.5 fusion.15
  35.7 0.8 add_convert_fusion
  36.6 0.5 maximum_bitcast_fusion
  37.1 0.0 copy-done
  37.1 8.3 %fusion.4 = f32[16,2,32,256]{2,3,1,0:T(8,128)} fusion(bf16[16,1,32,2,12,128]{5,2,4,3,1,0:T(8,128)(2,1)S(1)} %get-tuple-element.6, bf16[16,1,32,2,12,128]{5,2,4,3,1,0:T(8,128)(2,1)S(1)} %get-tuple-element.5, bf16[2,12,128,256]{3,2,1,0:T(8,128)(2,1)S(1)} %copy-done), kind=kOutput, calls=%fused_computation.8 | convolution fusion | flops 1613758464 | bytes 8912896 | tf_op jit(solution)/shard_map/dot_general | solution.py:32
  45.3 0.0 reduce-scatter.2.cloned.1.call-update
  45.4 177.2 %reduce-scatter.2.cloned.1.call-done = f32[16,2,32,8]{2,3,1,0:T(8,128)} async-done(((f32[16,2,32,256]{2,3,1,0:T(8,128)}), f32[16,2,32,8]{2,3,1,0:T(8,128)}) %reduce-scatter.2.cloned.1.call-update) | async-done | bytes 32784 | tf_op jit(solution)/shard_map/reduce_scatter | solution.py:45
  222.6 0.9 multiply_bitcast_fusion
  223.5 0.7 copy.26
  (1 shorter events, 0.0 us)
Async XLA Ops:
  6.5 30.5 %copy-start = (bf16[2,12,128,256]{3,2,1,0:T(8,128)(2,1)S(1)}, bf16[2,12,128,256]{3,2,1,0:T(8,128)(2,1)}, u32[]{:S(2)}) copy-start(bf16[2,12,128,256]{3,2,1,0:T(8,128)(2,1)} %param.4) | copy-start | bytes 4718596
  6.5 216.0 %reduce-scatter.2.cloned.1.call-start = ((), (), s32[]{:S(2)}) async-start(), calls=%async_computation.1 | async-start | bytes 4325376 | tf_op jit(solution)/shard_map/reduce_scatter | solution.py:45
Sparse Core Ops, SparseCore 0:
  45.5 177.0 reduce-scatter.1
where the time goes:
time: 231 us
  waiting for transfers between devices  177 us (77%)
  blocking collectives  27.4 us (12%)
  between operations  13.4 us (6%)
  matrix products  8.26 us (4%)
  other arithmetic  3.73 us (2%)
    reduce_scatter x1, waiting for transfers between devices, body(): lax.psum_scatter(partial_value, 'space', scatter_dimension=3, tiled=True)  177 us
    all_gather x1, blocking collectives, body(): lax.all_gather(right_modes, 'mode', axis=0, tiled=True)  27.4 us
    dot_general x1, matrix products, tile_terms(): lax.dot_general(stacked, left_mat, (((1,), (0,)), ((), ())), preferred_el...  8.26 us
  transfers between devices with their start and end apart: 1, of which 1 were waited for; matrix products, arithmetic and copies ran while one was open for 0% of the time, Pallas kernels for 0%

commit v1 on v0

--- a/solution.py
+++ b/solution.py
@@ -5,6 +5,13 @@
 from jax.sharding import PartitionSpec as P
 
 EXTENT = 96
+
+
+def gather_over(shard, name, dim):
+    size = lax.axis_size(name)
+    tiles = jnp.stack([shard for _ in range(size)])
+    tiles = lax.all_to_all(tiles, name, split_axis=0, concat_axis=0)
+    return jnp.concatenate(tiles, axis=dim)
 
 
 def phase_tables(momenta, coords):
@@ -39,9 +46,7 @@
     cosines, sines = phase_tables(momenta, coords)
     left_mat = left_modes.reshape(-1, left_modes.shape[-1])
     norm_scale = 1.0 / math.sqrt(12 * coords.shape[1] * lax.axis_size("space"))
-    partial_value = tile_terms(
-        left_mat, lax.all_gather(right_modes, "mode", axis=0, tiled=True), cosines, sines
-    )
+    partial_value = tile_terms(left_mat, gather_over(right_modes, "mode", 0), cosines, sines)
     owned = lax.psum_scatter(partial_value, "space", scatter_dimension=3, tiled=True)
     summed = jnp.transpose(owned, (3, 0, 1, 2))
     return summed * norm_scale

time: 231 us -> 222 us (0.961)
  blocking collectives: 27.4 us -> 0 us
  starting transfers between devices: 0.01 us -> 13.3 us
  waiting for transfers between devices: 177 us -> 181 us
    all_gather x1 -> x0, blocking collectives: 27.4 us -> none  [body(): lax.all_gather(right_modes, 'mode', axis=0, tiled=True)]
    all_to_all x0 -> x1, starting transfers between devices: none -> 13.2 us  [gather_over(): tiles = lax.all_to_all(tiles, name, split_axis=0, concat_axis=0)]
    all_to_all x0 -> x1, waiting for transfers between devices: none -> 8.23 us  [gather_over(): tiles = lax.all_to_all(tiles, name, split_axis=0, concat_axis=0)]
    reduce_scatter x1, waiting for transfers between devices: 177 us -> 172 us  [body(): lax.psum_scatter(partial_value, 'space', scatter_dimension=3, tiled=True)]
  transfers between devices with their start and end apart: 1 -> 2, of which waited for: 1 -> 2; matrix products, arithmetic and copies ran while one was open for 0% -> 0% of each run, Pallas kernels for 0% -> 0%
where the time goes in v1:
time: 222 us
  waiting for transfers between devices  181 us (82%)
  between operations  13.5 us (6%)
  starting transfers between devices  13.3 us (6%)
  matrix products  8.26 us (4%)
  other arithmetic  3.61 us (2%)
  local copies, waits for them, and re-layouts  2.48 us (1%)
    reduce_scatter x1, waiting for transfers between devices, body(): lax.psum_scatter(partial_value, 'space', scatter_dimension=3, tiled=True)  172 us
    all_to_all x1, starting transfers between devices, gather_over(): tiles = lax.all_to_all(tiles, name, split_axis=0, concat_axis=0)  13.2 us
    dot_general x1, matrix products, tile_terms(): lax.dot_general(stacked, left_mat, (((1,), (0,)), ((), ())), preferred_el...  8.26 us
    all_to_all x1, waiting for transfers between devices, gather_over(): tiles = lax.all_to_all(tiles, name, split_axis=0, concat_axis=0)  8.23 us
  transfers between devices with their start and end apart: 2, of which 2 were waited for; matrix products, arithmetic and copies ran while one was open for 0% of the time, Pallas kernels for 0%

profile of v1, /device:TPU:6, one launch (start us, length us, event | category | flops | bytes accessed | tf_op | source)
XLA Modules:
  0.0 221.8 jit_solution(4916182830126353037)
XLA Ops:
  6.5 0.0 copy-start
  6.5 0.8 copy.21
  7.4 0.8 stack.12
  8.2 13.2 %all-to-all-start = ((bf16[16,2,2,12,128]{4,1,3,2,0:T(2,128)(2,1)}), bf16[16,2,2,12,128]{4,1,3,2,0:T(2,128)(2,1)S(1)}, u32[]{:S(2)}, u32[]{:S(2)}) async-start(bf16[16,2,2,12,128]{4,1,3,2,0:T(2,128)(2,1)} %stack.12), calls=%async_computation | async-start | bytes 393216 | tf_op jit(solution)/shard_map/all_to_all | solution.py:13
  21.4 0.0 reduce-scatter.2.cloned.1.call-start
  21.4 0.8 multiply_reduce_fusion
  22.2 0.1 fusion.13
  22.3 8.2 %all-to-all-done = bf16[16,2,2,12,128]{4,1,3,2,0:T(2,128)(2,1)S(1)} async-done(((bf16[16,2,2,12,128]{4,1,3,2,0:T(2,128)(2,1)}), bf16[16,2,2,12,128]{4,1,3,2,0:T(2,128)(2,1)S(1)}, u32[]{:S(2)}, u32[]{:S(2)}) %all-to-all-start) | async-done | bytes 196640 | tf_op jit(solution)/shard_map/all_to_all | solution.py:13
  30.5 0.1 copy.22
  30.7 0.5 fusion.15
  31.2 0.8 add_convert_fusion
  32.0 0.5 maximum_bitcast_fusion
  32.5 0.0 copy-done
  32.6 8.3 %fusion.4 = f32[16,2,32,256]{2,3,1,0:T(8,128)} fusion(bf16[16,1,32,2,12,128]{5,2,4,3,1,0:T(8,128)(2,1)S(1)} %get-tuple-element.6, bf16[16,1,32,2,12,128]{5,2,4,3,1,0:T(8,128)(2,1)S(1)} %get-tuple-element.5, bf16[2,12,128,256]{3,2,1,0:T(8,128)(2,1)S(1)} %copy-done), kind=kOutput, calls=%fused_computation.8 | convolution fusion | flops 1613758464 | bytes 8912896 | tf_op jit(solution)/shard_map/dot_general | solution.py:39
  40.8 0.0 reduce-scatter.2.cloned.1.call-update
  40.8 172.5 %reduce-scatter.2.cloned.1.call-done = f32[16,2,32,8]{2,3,1,0:T(8,128)} async-done(((f32[16,2,32,256]{2,3,1,0:T(8,128)}), f32[16,2,32,8]{2,3,1,0:T(8,128)}) %reduce-scatter.2.cloned.1.call-update) | async-done | bytes 32784 | tf_op jit(solution)/shard_map/reduce_scatter | solution.py:50
  213.3 0.9 multiply_bitcast_fusion
  214.2 0.7 copy.25
  (1 shorter events, 0.0 us)
Async XLA Ops:
  6.5 26.0 %copy-start = (bf16[2,12,128,256]{3,2,1,0:T(8,128)(2,1)S(1)}, bf16[2,12,128,256]{3,2,1,0:T(8,128)(2,1)}, u32[]{:S(2)}) copy-start(bf16[2,12,128,256]{3,2,1,0:T(8,128)(2,1)} %param.4) | copy-start | bytes 4718596
  8.2 22.4 %all-to-all-start = ((bf16[16,2,2,12,128]{4,1,3,2,0:T(2,128)(2,1)}), bf16[16,2,2,12,128]{4,1,3,2,0:T(2,128)(2,1)S(1)}, u32[]{:S(2)}, u32[]{:S(2)}) async-start(bf16[16,2,2,12,128]{4,1,3,2,0:T(2,128)(2,1)} %stack.12), calls=%async_computation | async-start | bytes 393216 | tf_op jit(solution)/shard_map/all_to_all | solution.py:13
  21.4 191.9 %reduce-scatter.2.cloned.1.call-start = ((), (), s32[]{:S(2)}) async-start(), calls=%async_computation.2 | async-start | bytes 4325376 | tf_op jit(solution)/shard_map/reduce_scatter | solution.py:50
Sparse Core Ops, SparseCore 0:
  41.0 172.2 reduce-scatter.1
